TPU v7x, 32 devices: a whole 2x2x4 slice. The times are simulated.
32 devices in a mesh: groups: 2 (over y), req: 2 (over x), head: 4 (over z), sec: 2 (over core).
Axes of the slice: x: 2, y: 2, z: 4, core: 2. Of those that a mesh axis runs over, the one named last changes fastest.
Arguments:
- queries: bfloat16 [512, 4096], P(('groups', 'req'), ('head', 'sec')), parts along dimension 0, may hold values from -16 to 16
- cache_pool: bfloat16 [48, 128, 8, 128], P(('groups', 'req'), None, 'head'), parts along dimension 0, may hold values from -4 to 4
- lengths: int32 [4], P(('groups', 'req')), parts along dimension 0, may hold values from 128 to 1536, as said below
- block_table: int32 [4, 12], P(('groups', 'req')), parts along dimension 0, may hold values from 0 to 11, as said below
- out_proj: bfloat16 [4096, 2880], P(('head', 'sec')), may hold values from -0.375 to 0.375
- residual_in: bfloat16 [512, 2880], P(('groups', 'req', 'head', 'sec')), parts along dimension 0, may hold values from -16 to 16
- norm_gain: float32 [2880], replicated, may hold values from 0.1 to 1.9
- expert_ids: int32 [512, 4], P(('groups', 'req', 'head', 'sec')), parts along dimension 0, may hold values from 0 to 7, all different within a row; in each aligned block of 16 rows (0 to 15, 16 to 31, ...) at most 8 rows name the same one
- route_weight: float32 [512, 4], P(('groups', 'req', 'head', 'sec')), parts along dimension 0, may hold values from 0.2 to 1
- gate_weight: bfloat16 [8, 2880, 2880], P(('head', 'sec'), None, 'req'), may hold values from -0.109375 to 0.109375
- up_weight: bfloat16 [8, 2880, 2880], P(('head', 'sec'), None, 'req'), may hold values from -0.109375 to 0.109375
- down_weight: bfloat16 [8, 2880, 2880], P(('head', 'sec'), 'req'), may hold values from -0.109375 to 0.109375
Outputs:
- layer_out: bfloat16 [512, 2880], P(('groups', 'req', 'head', 'sec')), parts along dimension 0
There are 2 independent parts, one for each index of `groups`. A program takes and returns all parts, laid end to end along the dimension named above; an argument that names none is the same for every part. Nothing has to cross between parts.
Inputs may be any that keep to these rules, and one draw needn't show every extreme that they name: lengths[r] counts request r's positions, its last 128 positions being its new rows; some request reaches 1536 in every draw. `block_table`: each row is a permutation of 0 to 11. `expert_ids`: a row names 4 different experts; in each aligned block of 16 rows every expert is named by exactly 8 rows.
All inputs are finite; a program needn't handle non-finite values.
Results may differ from a plain program's by a relative error of at most 0.017.
Values may be sent and summed in bfloat16 or wider, within the bound.
A program may use at most 128 MiB of HBM per device.

v0:
```python
import math
import jax
import jax.numpy as jnp
from jax import lax
from jax.sharding import PartitionSpec as P

QH = 64
KVH = 8
TOP = 4
EPSILON = 1e-05
MASKED = -1e30


def run_expert(row_block, gate_weight, up_weight, down_weight):
    row_shape = row_block.shape
    flat_rows = row_block.reshape(-1, row_shape[-1])
    gate_out = jnp.dot(flat_rows, gate_weight[0], preferred_element_type=jnp.float32)
    up_out = jnp.dot(flat_rows, up_weight[0], preferred_element_type=jnp.float32)
    activated = (gate_out * jax.nn.sigmoid(1.702 * gate_out) * (up_out + 1.0)).astype(jnp.bfloat16)
    partial_value = jnp.dot(activated, down_weight[0], preferred_element_type=jnp.float32)
    return partial_value.astype(jnp.bfloat16).reshape(row_shape[:-1] + (partial_value.shape[-1],))


def masked_scores(query_heads, key_block, positions, score_scale):
    scores = (
        jnp.einsum("nhd,thd->hnt", query_heads, key_block, preferred_element_type=jnp.float32)
        * score_scale
    )
    key_positions = jnp.arange(key_block.shape[0], dtype=jnp.int32)
    visible = key_positions[None, None, :] <= positions[None, :, None]
    return jnp.where(visible, scores, MASKED)


def on_device(
    queries,
    cache_pool,
    lengths,
    block_table,
    out_proj,
    residual_in,
    norm_gain,
    expert_ids,
    route_weight,
    gate_weight,
    up_weight,
    down_weight,
):
    head_dim = cache_pool.shape[3] // 2
    block_len = cache_pool.shape[1]
    max_blocks = cache_pool.shape[0]
    new_rows = queries.shape[0]
    local_heads = queries.shape[1] // head_dim
    score_scale = 1.0 / math.sqrt(head_dim)
    context = lengths[0]
    sequence = cache_pool[block_table[0]]
    kv_choice = (
        lax.axis_index("sec") * local_heads + jnp.arange(local_heads, dtype=jnp.int32)
    ) // (QH // KVH)
    selected = jnp.take(sequence, kv_choice, axis=2)
    key_heads = selected[..., :head_dim]
    value_heads = selected[..., head_dim:]
    query_heads = queries.reshape(new_rows, local_heads, head_dim)
    positions = context - new_rows + jnp.arange(new_rows, dtype=jnp.int32)
    all_keys = key_heads.reshape(max_blocks * block_len, local_heads, head_dim)
    all_values = value_heads.reshape(max_blocks * block_len, local_heads, head_dim)
    scores = masked_scores(query_heads, all_keys, positions, score_scale)
    row_max = jnp.max(scores, axis=-1, keepdims=True)
    exp_scores = jnp.exp(scores - row_max)
    row_sum = jnp.sum(exp_scores, axis=-1, keepdims=True)
    probabilities = (exp_scores / row_sum).astype(jnp.bfloat16)
    attended = jnp.einsum(
        "hnt,thd->nhd", probabilities, all_values, preferred_element_type=jnp.float32
    )
    attn = attended.astype(jnp.bfloat16).reshape(new_rows, local_heads * head_dim)
    share_rows = new_rows // (lax.axis_size("head") * lax.axis_size("sec"))
    partial_value = jnp.dot(attn, out_proj, preferred_element_type=jnp.float32)
    projected = lax.psum_scatter(
        partial_value.astype(jnp.bfloat16).astype(jnp.float32).astype(jnp.bfloat16),
        ("head", "sec"),
        scatter_dimension=0,
        tiled=True,
    ).astype(jnp.float32)
    residual = (residual_in.astype(jnp.float32) + projected).astype(jnp.bfloat16)
    residual_wide = residual.astype(jnp.float32)
    mean_square = jnp.mean(residual_wide * residual_wide, axis=-1, keepdims=True)
    normed = (residual_wide * lax.rsqrt(mean_square + EPSILON) * norm_gain).astype(jnp.bfloat16)
    experts_all = lax.axis_size("head") * lax.axis_size("sec")
    capacity = share_rows * TOP // experts_all
    flat_ids = expert_ids.reshape(-1)
    onehot = (flat_ids[:, None] == jnp.arange(experts_all, dtype=jnp.int32)[None, :]).astype(
        jnp.int32
    )
    before = jnp.cumsum(onehot, axis=0) - onehot
    target = flat_ids * capacity + jnp.sum(before * onehot, axis=1)
    source_row = (
        jnp.zeros((experts_all * capacity,), jnp.int32)
        .at[target]
        .set(jnp.arange(share_rows * TOP, dtype=jnp.int32) // TOP)
    )
    buffer = normed[source_row].reshape(experts_all, capacity, normed.shape[1])
    copies = lax.all_gather(buffer[None], "req", axis=0, tiled=True)
    results = run_expert(
        lax.all_to_all(copies, ("head", "sec"), split_axis=1, concat_axis=1, tiled=True),
        gate_weight,
        up_weight,
        down_weight,
    )
    partial_back = lax.all_to_all(results, ("head", "sec"), split_axis=1, concat_axis=1, tiled=True)
    returned = (
        lax.psum_scatter(
            partial_back.astype(jnp.float32).astype(jnp.bfloat16),
            "req",
            scatter_dimension=0,
            tiled=True,
        )
        .astype(jnp.float32)[0]
        .astype(jnp.bfloat16)
    )
    gathered_out = returned.reshape(experts_all * capacity, -1)[target].reshape(share_rows, TOP, -1)
    expert_mix = jnp.sum(route_weight[:, :, None] * gathered_out.astype(jnp.float32), axis=1)
    return (residual.astype(jnp.float32) + expert_mix).astype(jnp.bfloat16)


def solution(mesh):
    return jax.shard_map(
        on_device,
        mesh=mesh,
        in_specs=(
            P(("groups", "req"), ("head", "sec")),
            P(("groups", "req"), None, "head", None),
            P(("groups", "req")),
            P(("groups", "req"), None),
            P(("head", "sec"), None),
            P(("groups", "req", "head", "sec"), None),
            P(),
            P(("groups", "req", "head", "sec"), None),
            P(("groups", "req", "head", "sec"), None),
            P(("head", "sec"), None, "req"),
            P(("head", "sec"), None, "req"),
            P(("head", "sec"), "req", None),
        ),
        out_specs=P(("groups", "req", "head", "sec"), None),
        check_vma=False,
    )
```

profile of v0, /device:TPU:0, one launch (start us, length us, event | category | flops | bytes accessed | tf_op | source)
XLA Modules:
  0.0 203.9 jit_solution(17053103708731632131)
XLA Ops:
  6.6 0.8 fusion.36
  7.4 4.3 %gather_fusion = bf16[12,128,2,128]{3,2,1,0:T(2,128)(2,1)} fusion(bf16[12,128,2,128]{3,2,1,0:T(2,128)(2,1)} %param.13, s32[1024]{0:T(1024)S(1)} %pad_clamp_fusion.3), kind=kCustom, calls=%fused_computation | custom fusion | bytes 1572912 | tf_op jit(solution)/shard_map/gather | solution.py:55
  11.7 2.2 %copy.61 = bf16[12,128,2,128]{3,1,2,0:T(8,128)(2,1)} copy(bf16[12,128,2,128]{3,2,1,0:T(2,128)(2,1)} %gather_fusion) | data formatting | bytes 1572864 | tf_op jit(solution)/shard_map/gather | solution.py:55
  13.9 3.7 %gather_fusion.1 = bf16[8,12,128,128]{3,2,1,0:T(8,128)(2,1)} fusion(bf16[12,128,2,128]{3,1,2,0:T(8,128)(2,1)} %copy.61, s32[1024]{0:T(1024)S(1)} %pad_clamp_fusion.2), kind=kCustom, calls=%fused_computation.1 | custom fusion | bytes 6291488 | tf_op jit(solution)/shard_map/jit(_take)/gather | solution.py:59
  17.6 2.3 %select_bitcast_fusion = bf16[12,128,8,128]{3,1,0,2:T(8,128)(2,1)S(1)} fusion(bf16[8,12,128,128]{3,2,1,0:T(8,128)(2,1)} %gather_fusion.1, pred[8]{0:T(512)(128)(4,1)S(1)} %compare_and_fusion), kind=kLoop, calls=%fused_computation.18 | loop fusion | flops 1572864 | bytes 6291464 | tf_op jit(solution)/shard_map/jit(_take)/select_n | solution.py:59
  19.9 0.0 copy-start.4
  19.9 3.8 %fusion.50 = (bf16[12,128,8,64]{3,1,0,2:T(8,128)(2,1)}, bf16[12,128,8,64]{3,1,0,2:T(8,128)(2,1)}) fusion(bf16[12,128,8,128]{3,1,0,2:T(8,128)(2,1)S(1)} %select_bitcast_fusion), kind=kLoop, calls=%fused_computation.82 | loop fusion | bytes 6291456 | tf_op jit(solution)/shard_map/slice | solution.py:60
  24.4 0.1 iota_compare_fusion
  24.6 0.1 copy.64
  24.7 4.1 %fusion.51 = f32[8,128]{1,0:T(8,128)S(1)} fusion(pred[128,1536]{0,1:T(8,128)(4,1)S(1)} %iota_compare_fusion, bf16[1536,8,64]{2,0,1:T(8,128)(2,1)} %bitcast.70, bf16[128,8,64]{0,2,1:T(8,128)(2,1)S(1)} %bitcast.75), kind=kOutput, calls=%fused_computation.83 | convolution fusion | flops 207619584 | bytes 1904640 | tf_op jit(solution)/shard_map/sub | solution.py:68
  28.7 5.8 %fusion.24 = bf16[8,64,128]{2,1,0:T(8,128)(2,1)S(1)} fusion(bf16[1536,8,64]{2,0,1:T(8,128)(2,1)} %bitcast.72, f32[8,128]{1,0:T(8,128)S(1)} %fusion.51, pred[128,1536]{0,1:T(8,128)(4,1)S(1)} %iota_compare_fusion, bf16[1536,8,64]{2,0,1:T(8,128)(2,1)} %bitcast.71, bf16[128,8,64]{0,2,1:T(8,128)(2,1)S(1)} %bitcast.76), kind=kOutput, calls=%fused_computation.26 | convolution fusion | flops 410585600 | bytes 3608576 | tf_op jit(solution)/shard_map/hnt,thd->nhd/dot_general | solution.py:71
  34.6 0.0 copy-start.6
  34.6 0.0 copy-start.2
  34.6 0.0 copy-start.5
  34.6 2.0 convolution_convert_fusion
  36.6 0.0 reduce-scatter.3.cloned.1.call-update
  36.6 0.0 all-reduce.3.cloned.1.call-start
  36.7 0.1 copy.68
  36.8 0.1 eq.15
  36.9 0.1 copy.67
  36.9 0.1 mul.82
  37.0 0.1 fusion.35
  37.1 0.1 reduce_window_sum.11
  37.2 0.2 select_reduce_fusion
  37.4 0.8 scatter_custom_fusion
  38.2 32.8 %reduce-scatter.3.cloned.1.call-done = bf16[16,2880]{1,0:T(8,128)(2,1)} async-done(((bf16[128,2880]{1,0:T(8,128)(2,1)}), bf16[16,2880]{1,0:T(8,128)(2,1)}) %reduce-scatter.3.cloned.1.call-update) | async-done | bytes 92176 | tf_op jit(solution)/shard_map/reduce_scatter | solution.py:77
  71.0 1.0 fusion.31
  72.0 1.0 fusion.33
  73.0 0.8 gather_fusion.2
  73.8 8.3 %all_gather.3 = bf16[2,8,8,2880]{3,2,1,0:T(8,128)(2,1)S(1)} all-gather(bf16[1,8,8,2880]{3,2,1,0:T(8,128)(2,1)S(1)} %bitcast.74), channel_id=1, replica_groups=mesh['groups'=2,'req'=2,'head'=4,'sec'=2] {'req'}, dimensions={0}, use_global_device_ids=true | all-gather | bytes 1105920 | tf_op jit(solution)/shard_map/all_gather | solution.py:101
  82.1 0.1 copy.69
  82.2 24.9 %all_to_all.10 = bf16[2,8,8,2880]{3,2,0,1:T(8,128)(2,1)S(1)} all-to-all(bf16[2,8,8,2880]{3,2,0,1:T(8,128)(2,1)S(1)} %copy.69), channel_id=1, replica_groups=mesh['groups'=2,'req'=2,'head'=4,'sec'=2] {'head','sec'}, dimensions={1} | all-to-all | bytes 1474560 | tf_op jit(solution)/shard_map/all_to_all | solution.py:103
  107.1 0.1 copy.70
  107.1 0.9 copy-done.1
  108.0 6.7 %fusion.5 = f32[128,1440]{0,1:T(8,128)} fusion(bf16[128,2880]{1,0:T(8,128)(2,1)S(1)} %bitcast.68, bf16[1,2880,1440]{1,2,0:T(8,128)(2,1)} %param.21), kind=kOutput, calls=%fused_computation.10 | convolution fusion | flops 1061683200 | bytes 9768960 | tf_op jit(solution)/shard_map/dot_general | solution.py:17
  114.7 15.6 %fusion.8 = bf16[128,2880]{0,1:T(8,128)(2,1)} fusion(bf16[1,1440,2880]{2,1,0:T(8,128)(2,1)} %param.23, bf16[128,2880]{1,0:T(8,128)(2,1)} %bitcast.69, bf16[1,2880,1440]{1,2,0:T(8,128)(2,1)} %param.22, f32[128,1440]{0,1:T(8,128)} %fusion.5), kind=kOutput, calls=%fused_computation.16 | convolution fusion | flops 2125209600 | bytes 18800640 | tf_op jit(solution)/shard_map/dot_general | solution.py:20
  130.3 2.3 %copy.71 = bf16[128,2880]{1,0:T(8,128)(2,1)} copy(bf16[128,2880]{0,1:T(8,128)(2,1)} %fusion.8) | data formatting | bytes 1474560 | tf_op jit(solution)/shard_map/convert_element_type | solution.py:21
  132.6 1.2 copy.72
  133.8 23.4 %all_to_all.11 = bf16[2,8,8,2880]{3,2,0,1:T(8,128)(2,1)} all-to-all(bf16[2,8,8,2880]{3,2,0,1:T(8,128)(2,1)S(1)} %copy.72), channel_id=1, replica_groups=mesh['groups'=2,'req'=2,'head'=4,'sec'=2] {'head','sec'}, dimensions={1} | all-to-all | bytes 1474560 | tf_op jit(solution)/shard_map/all_to_all | solution.py:108
  157.1 0.0 all-reduce.3.cloned.1.call-update
  157.2 0.1 copy.66
  157.3 0.6 dynamic-slice
  157.9 31.6 %all-reduce.3.cloned.1.call-done = bf16[2,8,8,2880]{3,2,0,1:T(8,128)(2,1)} async-done(((bf16[2,8,8,2880]{3,2,0,1:T(8,128)(2,1)}), bf16[2,8,8,2880]{3,2,0,1:T(8,128)(2,1)}) %all-reduce.3.cloned.1.call-update) | async-done | bytes 737296
  189.5 1.7 dynamic-slice_bitcast_fusion
  191.2 1.5 gather_fusion.3
  192.7 2.0 %reshape.195 = f32[16,4,2880]{2,1,0:T(4,128)} reshape(bf16[64,2880]{1,0:T(8,128)(2,1)} %gather_fusion.3) | data formatting | bytes 1105920 | tf_op jit(solution)/shard_map/convert_element_type | solution.py:120
  194.7 1.7 multiply_reduce_fusion
  196.4 0.7 fusion.34
  (26 shorter events, 0.1 us)
Async XLA Ops:
  6.5 28.1 %copy-start = (bf16[512,2880]{0,1:T(8,128)(2,1)S(1)}, bf16[512,2880]{0,1:T(8,128)(2,1)}, u32[]{:S(2)}) copy-start(bf16[512,2880]{0,1:T(8,128)(2,1)} %param.16) | copy-start | bytes 8847364
  6.5 64.5 %reduce-scatter.3.cloned.1.call-start = ((), (), s32[]{:S(2)}) async-start(), calls=%async_computation.3 | async-start | bytes 847872 | tf_op jit(solution)/shard_map/reduce_scatter | solution.py:77
  19.9 4.7 %copy-start.4 = (bf16[128,512]{1,0:T(8,128)(2,1)S(1)}, bf16[128,512]{1,0:T(8,128)(2,1)}, u32[]{:S(2)}) copy-start(bf16[128,512]{1,0:T(8,128)(2,1)} %param.12) | copy-start | bytes 393220
  34.6 2.1 %copy-start.6 = (s32[16,4]{0,1:T(4,128)S(1)}, s32[16,4]{0,1:T(4,128)}, u32[]{:S(2)}) copy-start(s32[16,4]{0,1:T(4,128)} %param.19) | copy-start | bytes 772
  34.6 36.4 %copy-start.2 = (bf16[16,2880]{1,0:T(8,128)(2,1)S(1)}, bf16[16,2880]{1,0:T(8,128)(2,1)}, u32[]{:S(2)}) copy-start(bf16[16,2880]{1,0:T(8,128)(2,1)} %param.17) | copy-start | bytes 276484
  34.6 37.5 %copy-start.5 = (f32[2880]{0:T(1024)S(1)}, f32[2880]{0:T(1024)}, u32[]{:S(2)}) copy-start(f32[2880]{0:T(1024)} %param.18) | copy-start | bytes 34564
  36.6 152.9 %all-reduce.3.cloned.1.call-start = ((), (), s32[]{:S(2)}) async-start(), calls=%async_computation.4 | async-start | bytes 1507328
  107.1 0.9 copy-start.1
  130.3 26.9 %copy-start.7 = (f32[16,4]{0,1:T(4,128)S(1)}, f32[16,4]{0,1:T(4,128)}, u32[]{:S(2)}) copy-start(f32[16,4]{0,1:T(4,128)} %param.20) | copy-start | bytes 772
  130.3 27.0 %copy-start.8 = (u32[32]{0:T(128)S(1)}, u32[32]{0:T(128)}, u32[]{:S(2)}) copy-start(u32[32]{0:T(128)} %constant.94) | copy-start | bytes 388
  157.2 39.2 %copy-start.3 = (bf16[16,2880]{1,0:T(8,128)(2,1)S(1)}, bf16[16,2880]{1,0:T(8,128)(2,1)}, u32[]{:S(2)}) copy-start(bf16[16,2880]{1,0:T(8,128)(2,1)} %reduce-scatter.3.cloned.1.call-done) | copy-start | bytes 276484
Sparse Core Ops, SparseCore 0:
  36.7 34.2 reduce-scatter.2
  157.3 32.1 all-reduce.2
where the time goes:
time: 205 us; the launch traced here: 204 us
  waiting for transfers between devices  64.4 us (31%)
  blocking collectives  56.5 us (28%)
  matrix products  34.2 us (17%)
  local copies, waits for them, and re-layouts  26.4 us (13%)
  between operations  14.3 us (7%)
  other arithmetic  7.99 us (4%)
    reduce_scatter x1, waiting for transfers between devices, on_device(): lax.psum_scatter(partial_value.astype(jnp.bfloat16).astype(jnp.float32).a...  32.8 us
    unnamed x3, waiting for transfers between devices  31.7 us
    all_to_all x1, blocking collectives, on_device(): lax.all_to_all(copies, ('head', 'sec'), split_axis=1, concat_axis=1, tile...  24.9 us
    all_to_all x1, blocking collectives, on_device(): lax.all_to_all(results, ('head', 'sec'), split_axis=1, concat_axis=1, til...  23.4 us
    dot_general x1, matrix products, run_expert(): jnp.dot(activated, down_weight[0], preferred_element_type=jnp.float32)  15.6 us
    all_gather x1, blocking collectives, on_device(): copies = lax.all_gather(buffer[None], 'req', axis=0, tiled=True)  8.28 us
    dot_general x1, matrix products, run_expert(): jnp.dot(flat_rows, gate_weight[0], preferred_element_type=jnp.float32)  6.69 us
    gather x2, local copies, waits for them, and re-layouts, on_device(): sequence = cache_pool[block_table[0]]  6.47 us
  transfers between devices with their start and end apart: 2, of which 2 were waited for; matrix products, arithmetic and copies ran while one was open for 1% of the time, Pallas kernels for 0%

commit v1 on v0

--- a/solution.py
+++ b/solution.py
@@ -9,6 +9,22 @@
 TOP = 4
 EPSILON = 1e-05
 MASKED = -1e30
+
+
+def pairwise_exchange(x, axis, split, join):
+    ways, here = (lax.axis_size(axis), lax.axis_index(axis))
+    width = x.shape[split] // ways
+    lengths = list(x.shape)
+    lengths[split] = width
+    height = lengths[join]
+    lengths[join] = height * ways
+    full = jnp.zeros(lengths, x.dtype)
+    for mask in range(ways):
+        part = lax.dynamic_slice_in_dim(x, (here ^ mask) * width, width, axis=split)
+        if mask:
+            part = lax.ppermute(part, axis, [(d, d ^ mask) for d in range(ways)])
+        full = lax.dynamic_update_slice_in_dim(full, part, (here ^ mask) * height, axis=join)
+    return full
 
 
 def run_expert(row_block, gate_weight, up_weight, down_weight):
@@ -105,7 +121,7 @@
         up_weight,
         down_weight,
     )
-    partial_back = lax.all_to_all(results, ("head", "sec"), split_axis=1, concat_axis=1, tiled=True)
+    partial_back = pairwise_exchange(results, ("head", "sec"), 1, 1)
     returned = (
         lax.psum_scatter(
             partial_back.astype(jnp.float32).astype(jnp.bfloat16),

time: 205 us -> 188 us (0.917)
  blocking collectives: 56.5 us -> 8.28 us
  starting transfers between devices: 0.04 us -> 13.1 us
  waiting for transfers between devices: 64.4 us -> 77.3 us
  local copies, waits for them, and re-layouts: 26.4 us -> 32.1 us
    all_to_all x2 -> x0, blocking collectives: 48.3 us -> none  [the longest x1 24.9 us: on_device(): lax.all_to_all(copies, ('head', 'sec'), split_axis=1, concat_axis=1, tile...]
    unnamed x3 -> x2, waiting for transfers between devices: 31.7 us -> 0.03 us
    all_to_all x0 -> x1, waiting for transfers between devices: none -> 20.1 us  [on_device(): lax.all_to_all(copies, ('head', 'sec'), split_axis=1, concat_axis=1, tile...]
    reduce_scatter x0 -> x1, waiting for transfers between devices: none -> 17.8 us  [on_device(): lax.psum_scatter(partial_back.astype(jnp.float32).astype(jnp.bfloat16), '...]
    ppermute x0 -> x7, starting transfers between devices: none -> 8.05 us  [pairwise_exchange(): part = lax.ppermute(part, axis, [(d, d ^ mask) for d in range(ways)])]
    ppermute x0 -> x7, waiting for transfers between devices: none -> 6.45 us  [pairwise_exchange(): part = lax.ppermute(part, axis, [(d, d ^ mask) for d in range(ways)])]
    all_to_all x0 -> x1, starting transfers between devices: none -> 4.82 us  [on_device(): lax.all_to_all(copies, ('head', 'sec'), split_axis=1, concat_axis=1, tile...]
    dynamic_update_slice x0 -> x7, local copies, waits for them, and re-layouts: none -> 4.56 us  [pairwise_exchange(): lax.dynamic_update_slice_in_dim(full, part, (here ^ mask) * height, axis=...]
  transfers between devices with their start and end apart: 2 -> 10, of which waited for: 2 -> 5; matrix products, arithmetic and copies ran while one was open for 1% -> 3% of each run, Pallas kernels for 0% -> 0%
where the time goes in v1:
time: 188 us; the launch traced here: 187 us
  waiting for transfers between devices  77.3 us (41%)
  matrix products  34.2 us (18%)
  local copies, waits for them, and re-layouts  32.1 us (17%)
  between operations  14.3 us (8%)
  starting transfers between devices  13.1 us (7%)
  blocking collectives  8.28 us (4%)
  other arithmetic  7.98 us (4%)
    reduce_scatter x1, waiting for transfers between devices, on_device(): lax.psum_scatter(partial_value.astype(jnp.bfloat16).astype(jnp.float32).a...  32.8 us
    all_to_all x1, waiting for transfers between devices, on_device(): lax.all_to_all(copies, ('head', 'sec'), split_axis=1, concat_axis=1, tile...  20.1 us
    reduce_scatter x1, waiting for transfers between devices, on_device(): lax.psum_scatter(partial_back.astype(jnp.float32).astype(jnp.bfloat16), '...  17.8 us
    dot_general x1, matrix products, run_expert(): jnp.dot(activated, down_weight[0], preferred_element_type=jnp.float32)  15.6 us
    all_gather x1, blocking collectives, on_device(): copies = lax.all_gather(buffer[None], 'req', axis=0, tiled=True)  8.28 us
    ppermute x7, starting transfers between devices, pairwise_exchange(): part = lax.ppermute(part, axis, [(d, d ^ mask) for d in range(ways)])  8.05 us
    dot_general x1, matrix products, run_expert(): jnp.dot(flat_rows, gate_weight[0], preferred_element_type=jnp.float32)  6.69 us
    gather x2, local copies, waits for them, and re-layouts, on_device(): sequence = cache_pool[block_table[0]]  6.47 us
  transfers between devices with their start and end apart: 10, of which 5 were waited for; matrix products, arithmetic and copies ran while one was open for 3% of the time, Pallas kernels for 0%

profile of v1, /device:TPU:0, one launch (start us, length us, event | category | flops | bytes accessed | tf_op | source)
XLA Modules:
  0.0 187.2 jit_solution(1635753682416524533)
XLA Ops:
  6.6 0.8 fusion.36
  7.4 4.3 %gather_fusion = bf16[12,128,2,128]{3,2,1,0:T(2,128)(2,1)} fusion(bf16[12,128,2,128]{3,2,1,0:T(2,128)(2,1)} %param.13, s32[1024]{0:T(1024)S(1)} %pad_clamp_fusion.3), kind=kCustom, calls=%fused_computation | custom fusion | bytes 1572912 | tf_op jit(solution)/shard_map/gather | solution.py:71
  11.7 2.2 %copy.55 = bf16[12,128,2,128]{3,1,2,0:T(8,128)(2,1)} copy(bf16[12,128,2,128]{3,2,1,0:T(2,128)(2,1)} %gather_fusion) | data formatting | bytes 1572864 | tf_op jit(solution)/shard_map/gather | solution.py:71
  13.9 3.7 %gather_fusion.1 = bf16[8,12,128,128]{3,2,1,0:T(8,128)(2,1)} fusion(bf16[12,128,2,128]{3,1,2,0:T(8,128)(2,1)} %copy.55, s32[1024]{0:T(1024)S(1)} %pad_clamp_fusion.2), kind=kCustom, calls=%fused_computation.1 | custom fusion | bytes 6291488 | tf_op jit(solution)/shard_map/jit(_take)/gather | solution.py:75
  17.6 2.3 %select_bitcast_fusion = bf16[12,128,8,128]{3,1,0,2:T(8,128)(2,1)S(1)} fusion(bf16[8,12,128,128]{3,2,1,0:T(8,128)(2,1)} %gather_fusion.1, pred[8]{0:T(512)(128)(4,1)S(1)} %compare_and_fusion), kind=kLoop, calls=%fused_computation.18 | loop fusion | flops 1572864 | bytes 6291464 | tf_op jit(solution)/shard_map/jit(_take)/select_n | solution.py:75
  19.9 3.8 %fusion.50 = (bf16[12,128,8,64]{3,1,0,2:T(8,128)(2,1)}, bf16[12,128,8,64]{3,1,0,2:T(8,128)(2,1)}) fusion(bf16[12,128,8,128]{3,1,0,2:T(8,128)(2,1)S(1)} %select_bitcast_fusion), kind=kLoop, calls=%fused_computation.96 | loop fusion | bytes 6291456 | tf_op jit(solution)/shard_map/slice | solution.py:76
  24.4 0.1 iota_compare_fusion
  24.6 0.1 copy.58
  24.7 4.1 %fusion.51 = f32[8,128]{1,0:T(8,128)S(1)} fusion(pred[128,1536]{0,1:T(8,128)(4,1)S(1)} %iota_compare_fusion, bf16[1536,8,64]{2,0,1:T(8,128)(2,1)} %bitcast.67, bf16[128,8,64]{0,2,1:T(8,128)(2,1)S(1)} %bitcast.72), kind=kOutput, calls=%fused_computation.97 | convolution fusion | flops 207619584 | bytes 1904640 | tf_op jit(solution)/shard_map/sub | solution.py:84
  28.7 5.8 %fusion.24 = bf16[8,64,128]{2,1,0:T(8,128)(2,1)S(1)} fusion(bf16[1536,8,64]{2,0,1:T(8,128)(2,1)} %bitcast.69, f32[8,128]{1,0:T(8,128)S(1)} %fusion.51, pred[128,1536]{0,1:T(8,128)(4,1)S(1)} %iota_compare_fusion, bf16[1536,8,64]{2,0,1:T(8,128)(2,1)} %bitcast.68, bf16[128,8,64]{0,2,1:T(8,128)(2,1)S(1)} %bitcast.73), kind=kOutput, calls=%fused_computation.26 | convolution fusion | flops 410585600 | bytes 3608576 | tf_op jit(solution)/shard_map/hnt,thd->nhd/dot_general | solution.py:87
  34.6 2.0 %convolution_convert_fusion = bf16[128,2880]{1,0:T(8,128)(2,1)} fusion(bf16[128,512]{0,1:T(8,128)(2,1)S(1)} %bitcast.74, bf16[512,2880]{0,1:T(8,128)(2,1)S(1)} %copy-done), kind=kOutput, calls=%fused_computation.17 | convolution fusion | flops 377856000 | bytes 3817472 | tf_op jit(solution)/shard_map/dot_general | solution.py:92
  37.1 0.1 reduce_window_sum.11
  37.2 0.2 select_reduce_fusion
  37.4 0.8 scatter_custom_fusion
  38.2 32.8 %reduce-scatter.3.cloned.1.call-done = bf16[16,2880]{1,0:T(8,128)(2,1)} async-done(((bf16[128,2880]{1,0:T(8,128)(2,1)}), bf16[16,2880]{1,0:T(8,128)(2,1)}) %reduce-scatter.3.cloned.1.call-update) | async-done | bytes 92176 | tf_op jit(solution)/shard_map/reduce_scatter | solution.py:93
  71.0 1.0 fusion.31
  72.0 1.0 fusion.33
  73.0 0.8 gather_fusion.2
  73.8 8.3 %all_gather.3 = bf16[2,8,8,2880]{3,2,1,0:T(8,128)(2,1)S(1)} all-gather(bf16[1,8,8,2880]{3,2,1,0:T(8,128)(2,1)S(1)} %bitcast.71), channel_id=1, replica_groups=mesh['groups'=2,'req'=2,'head'=4,'sec'=2] {'req'}, dimensions={0}, use_global_device_ids=true | all-gather | bytes 1105920 | tf_op jit(solution)/shard_map/all_gather | solution.py:117
  82.1 0.9 copy.63
  83.0 4.8 %all-to-all-start = ((bf16[2,8,8,2880]{3,2,0,1:T(8,128)(2,1)}), bf16[2,8,8,2880]{3,2,0,1:T(8,128)(2,1)}, u32[]{:S(2)}, u32[]{:S(2)}) async-start(bf16[2,8,8,2880]{3,2,0,1:T(8,128)(2,1)} %copy.63), calls=%async_computation.1 | async-start | bytes 1507328 | tf_op jit(solution)/shard_map/all_to_all | solution.py:119
  87.9 0.2 reduce-scatter.5.cloned.1.call-start
  88.1 20.1 %all-to-all-done = bf16[2,8,8,2880]{3,2,0,1:T(8,128)(2,1)} async-done(((bf16[2,8,8,2880]{3,2,0,1:T(8,128)(2,1)}), bf16[2,8,8,2880]{3,2,0,1:T(8,128)(2,1)}, u32[]{:S(2)}, u32[]{:S(2)}) %all-to-all-start) | async-done | bytes 737312 | tf_op jit(solution)/shard_map/all_to_all | solution.py:119
  108.2 1.2 copy.64
  109.4 0.9 copy-done.1
  110.3 6.7 %fusion.5 = f32[128,1440]{0,1:T(8,128)} fusion(bf16[128,2880]{1,0:T(8,128)(2,1)S(1)} %bitcast.65, bf16[1,2880,1440]{1,2,0:T(8,128)(2,1)} %param.21), kind=kOutput, calls=%fused_computation.10 | convolution fusion | flops 1061683200 | bytes 9768960 | tf_op jit(solution)/shard_map/dot_general | solution.py:33
  117.0 15.6 %fusion.8 = bf16[128,2880]{0,1:T(8,128)(2,1)} fusion(bf16[1,1440,2880]{2,1,0:T(8,128)(2,1)} %param.23, bf16[128,2880]{1,0:T(8,128)(2,1)} %bitcast.66, bf16[1,2880,1440]{1,2,0:T(8,128)(2,1)} %param.22, f32[128,1440]{0,1:T(8,128)} %fusion.5), kind=kOutput, calls=%fused_computation.16 | convolution fusion | flops 2125209600 | bytes 18800640 | tf_op jit(solution)/shard_map/dot_general | solution.py:36
  132.6 2.3 %copy.65 = bf16[128,2880]{1,0:T(8,128)(2,1)} copy(bf16[128,2880]{0,1:T(8,128)(2,1)} %fusion.8) | data formatting | bytes 1474560 | tf_op jit(solution)/shard_map/convert_element_type | solution.py:37
  134.9 0.9 broadcast_in_dim.43
  135.8 1.9 %constant_dynamic-slice_fusion.6 = (bf16[2,1,8,2880]{3,2,1,0:T(8,128)(2,1)S(1)}, bf16[2,1,8,2880]{3,2,1,0:T(8,128)(2,1)S(1)}, bf16[2,1,8,2880]{3,2,1,0:T(8,128)(...) fusion(bf16[2,8,8,2880]{3,2,1,0:T(8,128)(2,1)} %bitcast.70, ...), kind=kLoop, calls=%fused_computation.61 | loop fusion | bytes 1493024 | tf_op jit(solution)/shard_map/dynamic_slice | solution.py:23
  137.7 1.9 collective-permute-start.2
  139.6 0.1 collective-permute-start.3
  139.7 2.4 %collective-permute-start.4 = (bf16[2,1,8,2880]{3,2,1,0:T(8,128)(2,1)S(1)}, bf16[2,1,8,2880]{3,2,1,0:T(8,128)(2,1)S(1)}, u32[]{:S(2)}, u32[]{:S(2)}) collective-permute-start(bf16[2,1,8,2880]{3,2,1,0:T(8,128)(2,1)S(1)} %get-tuple-element.9), channel_id=1, source_target_pairs={{0,5},{1,4},{2,7},{3,6},{4,1},{5,0},{6,3},{7,2},{8,13},{9,12},{10,... | collective-permute-start | bytes 276488 | tf_op jit(solution)/shard_map/ppermute | solution.py:25
  142.1 1.3 collective-permute-start.5
  143.4 0.6 constant_dynamic-update-slice_fusion.5
  144.1 2.3 %collective-permute-start.6 = (bf16[2,1,8,2880]{3,2,1,0:T(8,128)(2,1)S(1)}, bf16[2,1,8,2880]{3,2,1,0:T(8,128)(2,1)S(1)}, u32[]{:S(2)}, u32[]{:S(2)}) collective-permute-start(bf16[2,1,8,2880]{3,2,1,0:T(8,128)(2,1)S(1)} %get-tuple-element.7), channel_id=1, source_target_pairs={{0,7},{1,6},{2,5},{3,4},{4,3},{5,2},{6,1},{7,0},{8,15},{9,14},{10,... | collective-permute-start | bytes 276488 | tf_op jit(solution)/shard_map/ppermute | solution.py:25
  146.4 0.6 constant_dynamic-update-slice_fusion.4
  147.1 0.7 constant_dynamic-update-slice_fusion.3
  147.7 6.4 %collective-permute-done.3 = bf16[2,1,8,2880]{3,2,1,0:T(8,128)(2,1)S(1)} collective-permute-done((bf16[2,1,8,2880]{3,2,1,0:T(8,128)(2,1)S(1)}, bf16[2,1,8,2880]{3,2,1,0:T(8,128)(2,1)S(1)}, u32[]{:S(2)}, u32[]{:S(2)}) %collective-permute-start.3) | collective-permute-done | bytes 92192 | tf_op jit(solution)/shard_map/ppermute | solution.py:25
  154.1 0.7 constant_dynamic-update-slice_fusion.2
  154.8 0.7 constant_dynamic-update-slice_fusion.1
  155.5 0.6 constant_dynamic-update-slice_fusion
  156.1 0.7 constant_dynamic-update-slice_fusion.6
  156.9 17.8 %reduce-scatter.5.cloned.1.call-done = bf16[1,8,8,2880]{3,2,1,0:T(8,128)(2,1)} async-done(((bf16[2,8,8,2880]{3,2,1,0:T(8,128)(2,1)}), bf16[1,8,8,2880]{3,2,1,0:T(8,128)(2,1)}) %reduce-scatter.5.cloned.1.call-update) | async-done | bytes 368656 | tf_op jit(solution)/shard_map/reduce_scatter | solution.py:126
  174.7 2.2 %gather_fusion.3 = bf16[64,2880]{1,0:T(8,128)(2,1)S(1)} fusion(bf16[64,2880]{1,0:T(8,128)(2,1)} %bitcast.64, s32[1024]{0:T(1024)S(1)} %pad_clamp_fusion), kind=kCustom, calls=%fused_computation.3 | custom fusion | bytes 737536 | tf_op jit(solution)/shard_map/gather | solution.py:135
  176.9 1.1 reshape.195
  178.0 1.7 multiply_reduce_fusion
  179.7 0.7 fusion.34
  (44 shorter events, 0.7 us)
Async XLA Ops:
  6.5 28.1 %copy-start = (bf16[512,2880]{0,1:T(8,128)(2,1)S(1)}, bf16[512,2880]{0,1:T(8,128)(2,1)}, u32[]{:S(2)}) copy-start(bf16[512,2880]{0,1:T(8,128)(2,1)} %param.16) | copy-start | bytes 8847364
  6.5 64.5 %reduce-scatter.3.cloned.1.call-start = ((), (), s32[]{:S(2)}) async-start(), calls=%async_computation.3 | async-start | bytes 847872 | tf_op jit(solution)/shard_map/reduce_scatter | solution.py:93
  19.9 4.7 %copy-start.4 = (bf16[128,512]{1,0:T(8,128)(2,1)S(1)}, bf16[128,512]{1,0:T(8,128)(2,1)}, u32[]{:S(2)}) copy-start(bf16[128,512]{1,0:T(8,128)(2,1)} %param.12) | copy-start | bytes 393220
  34.6 2.1 %copy-start.6 = (s32[16,4]{0,1:T(4,128)S(1)}, s32[16,4]{0,1:T(4,128)}, u32[]{:S(2)}) copy-start(s32[16,4]{0,1:T(4,128)} %param.19) | copy-start | bytes 772
  34.6 36.4 %copy-start.2 = (bf16[16,2880]{1,0:T(8,128)(2,1)S(1)}, bf16[16,2880]{1,0:T(8,128)(2,1)}, u32[]{:S(2)}) copy-start(bf16[16,2880]{1,0:T(8,128)(2,1)} %param.17) | copy-start | bytes 276484
  34.6 37.5 %copy-start.5 = (f32[2880]{0:T(1024)S(1)}, f32[2880]{0:T(1024)}, u32[]{:S(2)}) copy-start(f32[2880]{0:T(1024)} %param.18) | copy-start | bytes 34564
  83.0 25.2 %all-to-all-start = ((bf16[2,8,8,2880]{3,2,0,1:T(8,128)(2,1)}), bf16[2,8,8,2880]{3,2,0,1:T(8,128)(2,1)}, u32[]{:S(2)}, u32[]{:S(2)}) async-start(bf16[2,8,8,2880]{3,2,0,1:T(8,128)(2,1)} %copy.63), calls=%async_computation.1 | async-start | bytes 1507328 | tf_op jit(solution)/shard_map/all_to_all | solution.py:119
  87.9 86.9 %reduce-scatter.5.cloned.1.call-start = ((), (), s32[]{:S(2)}) async-start(), calls=%async_computation.4 | async-start | bytes 1130496 | tf_op jit(solution)/shard_map/reduce_scatter | solution.py:126
  109.4 0.9 copy-start.1
  132.6 24.2 %copy-start.7 = (f32[16,4]{0,1:T(4,128)S(1)}, f32[16,4]{0,1:T(4,128)}, u32[]{:S(2)}) copy-start(f32[16,4]{0,1:T(4,128)} %param.20) | copy-start | bytes 772
  137.7 4.4 %collective-permute-start = (bf16[2,1,8,2880]{3,2,1,0:T(8,128)(2,1)S(1)}, bf16[2,1,8,2880]{3,2,1,0:T(8,128)(2,1)S(1)}, u32[]{:S(2)}, u32[]{:S(2)}) collective-permute-start(bf16[2,1,8,2880]{3,2,1,0:T(8,128)(2,1)S(1)} %get-tuple-element.13), channel_id=1, source_target_pairs={{0,1},{1,0},{2,3},{3,2},{4,5},{5,4},{6,7},{7,6},{8,9},{9,8},{10,11... | collective-permute-start | bytes 276488 | tf_op jit(solution)/shard_map/ppermute | solution.py:25
  137.7 6.4 %collective-permute-start.1 = (bf16[2,1,8,2880]{3,2,1,0:T(8,128)(2,1)S(1)}, bf16[2,1,8,2880]{3,2,1,0:T(8,128)(2,1)S(1)}, u32[]{:S(2)}, u32[]{:S(2)}) collective-permute-start(bf16[2,1,8,2880]{3,2,1,0:T(8,128)(2,1)S(1)} %get-tuple-element.12), channel_id=1, source_target_pairs={{0,2},{1,3},{2,0},{3,1},{4,6},{5,7},{6,4},{7,5},{8,10},{9,11},{10,... | collective-permute-start | bytes 276488 | tf_op jit(solution)/shard_map/ppermute | solution.py:25
  137.7 9.3 %collective-permute-start.2 = (bf16[2,1,8,2880]{3,2,1,0:T(8,128)(2,1)S(1)}, bf16[2,1,8,2880]{3,2,1,0:T(8,128)(2,1)S(1)}, u32[]{:S(2)}, u32[]{:S(2)}) collective-permute-start(bf16[2,1,8,2880]{3,2,1,0:T(8,128)(2,1)S(1)} %get-tuple-element.11), channel_id=1, source_target_pairs={{0,3},{1,2},{2,1},{3,0},{4,7},{5,6},{6,5},{7,4},{8,11},{9,10},{10,... | collective-permute-start | bytes 276488 | tf_op jit(solution)/shard_map/ppermute | solution.py:25
  139.6 14.5 %collective-permute-start.3 = (bf16[2,1,8,2880]{3,2,1,0:T(8,128)(2,1)S(1)}, bf16[2,1,8,2880]{3,2,1,0:T(8,128)(2,1)S(1)}, u32[]{:S(2)}, u32[]{:S(2)}) collective-permute-start(bf16[2,1,8,2880]{3,2,1,0:T(8,128)(2,1)S(1)} %get-tuple-element.10), channel_id=1, source_target_pairs={{0,4},{1,5},{2,6},{3,7},{4,0},{5,1},{6,2},{7,3},{8,12},{9,13},{10,... | collective-permute-start | bytes 276488 | tf_op jit(solution)/shard_map/ppermute | solution.py:25
  139.7 15.1 %collective-permute-start.4 = (bf16[2,1,8,2880]{3,2,1,0:T(8,128)(2,1)S(1)}, bf16[2,1,8,2880]{3,2,1,0:T(8,128)(2,1)S(1)}, u32[]{:S(2)}, u32[]{:S(2)}) collective-permute-start(bf16[2,1,8,2880]{3,2,1,0:T(8,128)(2,1)S(1)} %get-tuple-element.9), channel_id=1, source_target_pairs={{0,5},{1,4},{2,7},{3,6},{4,1},{5,0},{6,3},{7,2},{8,13},{9,12},{10,... | collective-permute-start | bytes 276488 | tf_op jit(solution)/shard_map/ppermute | solution.py:25
  142.1 13.4 %collective-permute-start.5 = (bf16[2,1,8,2880]{3,2,1,0:T(8,128)(2,1)S(1)}, bf16[2,1,8,2880]{3,2,1,0:T(8,128)(2,1)S(1)}, u32[]{:S(2)}, u32[]{:S(2)}) collective-permute-start(bf16[2,1,8,2880]{3,2,1,0:T(8,128)(2,1)S(1)} %get-tuple-element.8), channel_id=1, source_target_pairs={{0,6},{1,7},{2,4},{3,5},{4,2},{5,3},{6,0},{7,1},{8,14},{9,15},{10,... | collective-permute-start | bytes 276488 | tf_op jit(solution)/shard_map/ppermute | solution.py:25
  144.1 12.0 %collective-permute-start.6 = (bf16[2,1,8,2880]{3,2,1,0:T(8,128)(2,1)S(1)}, bf16[2,1,8,2880]{3,2,1,0:T(8,128)(2,1)S(1)}, u32[]{:S(2)}, u32[]{:S(2)}) collective-permute-start(bf16[2,1,8,2880]{3,2,1,0:T(8,128)(2,1)S(1)} %get-tuple-element.7), channel_id=1, source_target_pairs={{0,7},{1,6},{2,5},{3,4},{4,3},{5,2},{6,1},{7,0},{8,15},{9,14},{10,... | collective-permute-start | bytes 276488 | tf_op jit(solution)/shard_map/ppermute | solution.py:25
  156.8 22.9 %copy-start.3 = (bf16[16,2880]{1,0:T(8,128)(2,1)S(1)}, bf16[16,2880]{1,0:T(8,128)(2,1)}, u32[]{:S(2)}) copy-start(bf16[16,2880]{1,0:T(8,128)(2,1)} %reduce-scatter.3.cloned.1.call-done) | copy-start | bytes 276484
Sparse Core Ops, SparseCore 0:
  36.7 34.2 reduce-scatter.2
  156.9 17.7 reduce-scatter.4
